TPU v7x, 32 devices: a whole 2x2x4 slice. The times are simulated.
32 devices in a mesh: mem: 4 (over z), lat: 8 (over y, x, core).
Axes of the slice: x: 2, y: 2, z: 4, core: 2. Of those that a mesh axis runs over, the one named last changes fastest.
Arguments:
- features: bfloat16 [16, 16, 1440, 128], P('mem', 'lat'), may hold values from -6 to 6
- conv_inner: bfloat16 [3, 3, 128, 128], replicated, may hold values from -0.1875 to 0.1875
- conv_head: bfloat16 [3, 3, 128, 69], replicated, may hold values from -0.1875 to 0.1875
- truth: float32 [69, 16, 1440], P(None, 'lat'), may hold values from -5 to 5
- kernel_width: float32 [69], replicated, may hold values from 0.3 to 1.5
- var_weight: float32 [69], replicated, may hold values from 0.5 to 2
Outputs:
- grad_features: bfloat16 [16, 16, 1440, 128], P('mem', 'lat')
- grad_inner: float32 [3, 3, 128, 128], replicated
- grad_head: float32 [3, 3, 128, 69], replicated
All inputs are finite; a program needn't handle non-finite values.
Results may differ from a plain program's by a relative error of at most 0.0098.
Values may be sent and summed in bfloat16 or wider, within the bound.
No kernel may reach another device: no remote copies, remote signals or barrier semaphores. Data moves between devices by JAX's collectives and lax.ppermute only.
A program may use at most 256 MiB of HBM per device.

v0:
```python
import jax
import jax.numpy as jnp
from jax import lax
from jax.sharding import PartitionSpec as P


def padded_2(cells, sides, width):
    for axis, dim in sides:
        count = lax.axis_size(axis)
        ends = count - 1
        head = lax.slice_in_dim(cells, 0, width, axis=dim)
        tail = lax.slice_in_dim(cells, cells.shape[dim] - width, cells.shape[dim], axis=dim)
        cells = jnp.concatenate(
            [
                lax.ppermute(tail, axis, [(i, (i + 1) % count) for i in range(ends)]),
                cells,
                lax.ppermute(head, axis, [((i + 1) % count, i) for i in range(ends)]),
            ],
            axis=dim,
        )
    return cells


def wrap_lon(values, axis):
    count = values.shape[axis]
    return jnp.concatenate(
        [
            lax.slice_in_dim(values, count - 1, count, axis=axis),
            values,
            lax.slice_in_dim(values, 0, 1, axis=axis),
        ],
        axis=axis,
    )


def gelu_slope(pre):
    return jax.jvp(jax.nn.gelu, (pre,), (jnp.ones_like(pre),))[1]


def hidden_conv(padded, kernel, band_rows):
    lon_cells = padded.shape[2] - 2
    summed = jnp.zeros((padded.shape[0], band_rows, lon_cells, kernel.shape[3]), jnp.float32)
    for row_off in range(3):
        for col_off in range(3):
            summed = summed + jnp.einsum(
                "mrlc,co->mrlo",
                padded[:, row_off : row_off + band_rows, col_off : col_off + lon_cells],
                kernel[row_off, col_off],
                preferred_element_type=jnp.float32,
            )
    return summed


def field_conv(padded, kernel, band_rows):
    lon_cells = padded.shape[2] - 2
    summed = jnp.zeros((padded.shape[0], kernel.shape[3], band_rows, lon_cells), jnp.float32)
    for row_off in range(3):
        for col_off in range(3):
            summed = summed + jnp.einsum(
                "mrlc,cv->mvrl",
                padded[:, row_off : row_off + band_rows, col_off : col_off + lon_cells],
                kernel[row_off, col_off],
                preferred_element_type=jnp.float32,
            )
    return summed


def field_back(padded_grad, kernel, band_rows):
    lon_cells = padded_grad.shape[3] - 2
    summed = jnp.zeros((padded_grad.shape[0], band_rows, lon_cells, kernel.shape[2]), jnp.float32)
    for row_off in range(3):
        for col_off in range(3):
            summed = summed + jnp.einsum(
                "mvrl,cv->mrlc",
                padded_grad[
                    :,
                    :,
                    2 - row_off : 2 - row_off + band_rows,
                    2 - col_off : 2 - col_off + lon_cells,
                ],
                kernel[row_off, col_off],
                preferred_element_type=jnp.float32,
            )
    return summed


def hidden_back(padded_grad, kernel, band_rows):
    lon_cells = padded_grad.shape[2] - 2
    summed = jnp.zeros((padded_grad.shape[0], band_rows, lon_cells, kernel.shape[2]), jnp.float32)
    for row_off in range(3):
        for col_off in range(3):
            summed = summed + jnp.einsum(
                "mrlo,co->mrlc",
                padded_grad[
                    :, 2 - row_off : 2 - row_off + band_rows, 2 - col_off : 2 - col_off + lon_cells
                ],
                kernel[row_off, col_off],
                preferred_element_type=jnp.float32,
            )
    return summed


def kernel_grad(padded_input, grad_out, form, band_rows, lon_cells):
    pieces = []
    for row_off in range(3):
        for col_off in range(3):
            pieces.append(
                jnp.einsum(
                    form,
                    padded_input[:, row_off : row_off + band_rows, col_off : col_off + lon_cells],
                    grad_out,
                    preferred_element_type=jnp.float32,
                )
            )
    return jnp.stack(pieces).reshape((3, 3) + pieces[0].shape)


def pair_sums(own, others, inverse):
    spread = others[None] - own[:, None]
    kernel = jnp.exp(-0.5 * spread * spread * inverse[None, None, :, None, None])
    return jnp.sum(kernel * spread, axis=1)


def member_grad(own, pairwise, truth_piece, inverse, var_weight, members):
    offset = own - truth_piece[None]
    nearness = jnp.exp(-0.5 * offset * offset * inverse[None, :, None, None])
    scale = (var_weight * inverse)[None, :, None, None]
    return scale * (2.0 / (members - 1) * pairwise + 2.0 * nearness * offset)


def split_groups(values, blocks, group):
    shaped = values.reshape((values.shape[0], blocks, group) + values.shape[2:])
    return jnp.moveaxis(shaped, 1, 0)


def shards(features, conv_inner, conv_head, truth, kernel_width, var_weight):
    band_rows = features.shape[1]
    lon_cells = features.shape[2]
    variables = conv_head.shape[3]
    feature_ext = padded_2(features, (("lat", 1),), 1)
    pre_own = hidden_conv(wrap_lon(feature_ext, 2), conv_inner, band_rows)
    hidden_own = jax.nn.gelu(pre_own).astype(jnp.bfloat16)
    hidden_ext = padded_2(hidden_own, (("lat", 1),), 1)
    hidden_wrap = wrap_lon(hidden_ext, 2)
    field = field_conv(hidden_wrap, conv_head, band_rows).astype(jnp.bfloat16)
    inverse = 1.0 / (kernel_width * kernel_width)
    group = 3
    blocks = variables // group
    inverse_blocks = inverse.reshape(blocks, group)
    gathered = lax.all_to_all(field, "mem", split_axis=3, concat_axis=0, tiled=True)
    values = gathered.astype(jnp.float32)
    members = values.shape[0]
    piece_cells = values.shape[3]

    def block_pairs(packed):
        member_values, rates = packed
        return pair_sums(member_values, member_values, rates)

    pairwise = lax.map(block_pairs, (split_groups(values, blocks, group), inverse_blocks))
    pairwise = jnp.moveaxis(pairwise, 0, 1).reshape(values.shape)
    truth_piece = lax.dynamic_slice_in_dim(
        truth, lax.axis_index("mem") * piece_cells, piece_cells, 2
    )
    gradient = member_grad(values, pairwise, truth_piece, inverse, var_weight, members).astype(
        jnp.bfloat16
    )
    field_grad = lax.all_to_all(gradient, "mem", split_axis=0, concat_axis=3, tiled=True)
    grad_pad = padded_2(field_grad, (("lat", 2),), 1)
    hidden_grad = (
        field_back(wrap_lon(grad_pad, 3), conv_head, band_rows) * gelu_slope(pre_own)
    ).astype(jnp.bfloat16)
    head_grad = kernel_grad(hidden_wrap, field_grad, "mrlc,mvrl->cv", band_rows, lon_cells)
    hidden_pad = padded_2(hidden_grad, (("lat", 1),), 1)
    grad_features = hidden_back(wrap_lon(hidden_pad, 2), conv_inner, band_rows).astype(jnp.bfloat16)
    inner_grad = kernel_grad(
        wrap_lon(feature_ext, 2), hidden_grad, "mrlc,mrlo->co", band_rows, lon_cells
    )
    inner_sum, head_sum = lax.psum((inner_grad, head_grad), ("mem", "lat"))
    points = band_rows * lax.axis_size("lat") * lon_cells
    return (grad_features, inner_sum / points, head_sum / points)


def solution(mesh):
    in_specs = (P("mem", "lat", None, None), P(), P(), P(None, "lat", None), P(), P())
    out_specs = (P("mem", "lat", None, None), P(), P())
    return jax.shard_map(shards, mesh=mesh, in_specs=in_specs, out_specs=out_specs, check_vma=False)
```

profile of v0, /device:TPU:0, one launch (start us, length us, event | category | flops | bytes accessed | tf_op | source)
XLA Modules:
  0.0 686.2 jit_solution(3638382335253527599)
XLA Ops:
  13.2 3.5 fusion.177
  19.7 4.1 fusion.183
  23.7 4.0 fusion.173
  31.1 3.4 fusion.163
  34.5 3.4 fusion.180
  44.7 21.2 %multiply_convert_fusion = (bf16[4,2,1440,128]{3,2,1,0:T(8,128)(2,1)}, f32[4,2,1440,128]{3,2,1,0:T(8,128)}) fusion(bf16[3,3,128,128]{3,2,1,0:T(8,128)(2,1)S(1)} %copy-done.21, bf16[4,4,1,128]{3,2,1,0:T(2,128)(2,1)S(1)} %get-tuple-element.58, bf16[4,4,1440,128]{3,2,1,0:T(8,128)(2,1)} %copy-done.2, f32[4,2,1440,128]{3,2,1,0:T(8,128)} %fusion.168, ...), kind=kOutput, calls=%fused_computation.41 | convolution fusion | flops 408453120 | bytes 61972480 | tf_op jit(solution)/shard_map/mrlc,co->mrlo/dot_general | solution.py:45
  68.1 30.4 %collective-permute-start.2 = (bf16[4,1,1440,128]{3,2,1,0:T(8,128)(2,1)S(1)}, bf16[4,1,1440,128]{3,2,1,0:T(8,128)(2,1)S(1)}, u32[]{:S(2)}, u32[]{:S(2)}) collective-permute-start(bf16[4,1,1440,128]{3,2,1,0:T(8,128)(2,1)S(1)} %get-tuple-element.64), channel_id=1, source_target_pairs={{0,1},{1,2},{2,3},{3,4},{4,5},{5,6},{6,7},{8,9},{9,10},{10,11},{11... | collective-permute-start | bytes 4423688 | tf_op jit(solution)/shard_map/ppermute | solution.py:15
  103.7 7.3 %fusion.7 = (bf16[4,4,1441,128]{3,2,1,0:T(8,128)(2,1)S(1)}, bf16[4,4,1441,128]{3,2,1,0:T(8,128)(2,1)S(1)}) fusion(bf16[4,1,1440,128]{3,2,1,0:T(8,128)(2,1)S(1)} %collective-permute-done.3, bf16[4,2,1440,128]{3,2,1,0:T(8,128)(2,1)S(1)} %copy-done.5, bf16[4,1,1440,128]{3,2,1,0:T(8,128)(2,1)S(1)} %collective-permute-done.2), kind=kLoop, calls=%fused_computation.26 | loop fusion | flops 70828032 | bytes 17702912 | tf_op jit(solution)/shard_map/concatenate | solution.py:26
  111.0 4.1 fusion.76
  115.1 3.6 fusion.84
  118.7 3.6 fusion.92
  122.3 3.6 fusion.80
  126.0 3.6 fusion.88
  133.2 8.2 %fusion.71 = bf16[4,69,2,1440]{3,1,2,0:T(8,128)(2,1)} fusion(bf16[4,4,1441,128]{3,2,1,0:T(8,128)(2,1)S(1)} %get-tuple-element.57, f32[4,2,1440,69]{2,3,1,0:T(8,128)S(1)} %fusion.53, f32[4,2,1440,69]{2,3,1,0:T(8,128)} %fusion.76, f32[4,2,1440,69]{2,3,1,0:T(8,128)} %fusion.80, f32[4,2,1440,69]{2,3,1,0:T(8,128)S(1)} %fusion.218, ...), kind=kOutput, calls=%fused_computation.109 | convolution fusion | flops 210643200 | bytes 32868864 | tf_op jit(solution)/shard_map/mrlc,cv->mvrl/dot_general | solution.py:59
  141.4 8.4 %copy.54 = bf16[4,69,2,1440]{1,2,0,3:T(2,128)(2,1)} copy(bf16[4,69,2,1440]{3,1,2,0:T(8,128)(2,1)} %fusion.71) | data formatting | bytes 3179520 | tf_op jit(solution)/shard_map/convert_element_type | solution.py:145
  149.8 4.9 all-to-all-start
  155.2 46.0 %all-to-all-done = bf16[4,69,2,1440]{1,2,0,3:T(2,128)(2,1)} async-done(((bf16[4,69,2,1440]{1,2,0,3:T(2,128)(2,1)}), bf16[4,69,2,1440]{1,2,0,3:T(2,128)(2,1)}, u32[]{:S(2)}, u32[]{:S(2)}) %all-to-all-start) | async-done | bytes 1589792 | tf_op jit(solution)/shard_map/all_to_all | solution.py:150
  201.1 7.7 %copy.55 = bf16[4,69,2,1440]{3,0,2,1:T(4,128)(2,1)S(1)} copy(bf16[4,69,2,1440]{1,2,0,3:T(2,128)(2,1)} %all-to-all-done) | data formatting | bytes 3179520 | tf_op jit(solution)/shard_map/all_to_all | solution.py:150
  208.9 3.8 reshape.78
  212.7 5.6 copy.57
  218.3 3.7 copy.60
  222.1 61.3 %while.10 = (s32[]{:T(128)}, f32[23,16,3,2,360]{4,1,3,2,0:T(8,128)}, f32[23,16,3,2,360]{4,3,2,0,1:T(2,128)}, f32[23,3]{1,0:T(8,128)S(1)}, s32[]{:T(128)}) while((s32[]{:T(128)}, f32[23,16,3,2,360]{4,1,3,2,0:T(8,128)}, f32[23,16,3,2,360]{4,3,2,0,1:T(2,128)}, f32[23,3]{1,0:T(8,128)S(1)}, s32[]{:T(128)}) %tuple.48), condition=%wide.region_2.3_spmd, body=%wide.region_0.2_spmd.sunk | while | flops 3283202 | bytes 1253493 | solution.py:159
  291.0 25.7 %all_to_all.27 = bf16[16,69,2,360]{3,2,1,0:T(2,128)(2,1)S(1)} all-to-all(bf16[16,69,2,360]{3,2,1,0:T(2,128)(2,1)S(1)} %copy.62), channel_id=1, replica_groups=mesh['mem'=4,'lat'=8] {'mem'}, dimensions={0} | all-to-all | bytes 3179520 | tf_op jit(solution)/shard_map/all_to_all | solution.py:167
  319.5 3.5 all_to_all.24
  334.7 22.2 %collective-permute-start.4 = (bf16[4,69,1,1440]{3,0,2,1:T(4,128)(2,1)S(1)}, bf16[4,69,1,1440]{3,0,2,1:T(4,128)(2,1)S(1)}, u32[]{:S(2)}, u32[]{:S(2)}) collective-permute-start(bf16[4,69,1,1440]{3,0,2,1:T(4,128)(2,1)S(1)} %copy.65), channel_id=1, source_target_pairs={{0,1},{1,2},{2,3},{3,4},{4,5},{5,6},{6,7},{8,9},{9,10},{10,11},{11... | collective-permute-start | bytes 2384648 | tf_op jit(solution)/shard_map/ppermute | solution.py:15
  360.5 3.5 fusion.216
  364.4 43.1 %collective-permute-done.5 = bf16[4,69,1,1440]{3,0,2,1:T(4,128)(2,1)S(1)} collective-permute-done((bf16[4,69,1,1440]{3,0,2,1:T(4,128)(2,1)S(1)}, bf16[4,69,1,1440]{3,0,2,1:T(4,128)(2,1)S(1)}, u32[]{:S(2)}, u32[]{:S(2)}) %collective-permute-start.5) | collective-permute-done | bytes 794912 | tf_op jit(solution)/shard_map/ppermute | solution.py:17
  407.8 4.2 fusion.98
  412.0 4.2 fusion.95
  416.3 4.1 fusion.104
  420.4 4.1 fusion.108
  424.5 4.2 fusion.101
  428.6 4.0 fusion.57
  432.6 3.6 fusion.61
  436.2 21.4 %fusion.19 = bf16[4,2,1440,128]{3,2,1,0:T(8,128)(2,1)} fusion(f32[4,2,1440,128]{3,2,1,0:T(8,128)} %get-tuple-element.82, f32[4,2,1440,128]{3,2,1,0:T(8,128)} %fusion.61, f32[4,2,1440,128]{3,2,1,0:T(8,128)} %fusion.108, f32[4,2,1440,128]{3,2,1,0:T(8,128)} %fusion.95, f32[4,2,1440,128]{3,2,1,0:T(8,128)} %fusion.216, f32[4,2,1440,128]{3,2,1,0:T(8,128)} %fusion.101, ...), kind=kOutput, calls=%fused_computation.39 | convolution fusion | flops 245007360 | bytes 59526144 | tf_op jit(solution)/shard_map/mvrl,cv->mrlc/dot_general | solution.py:73
  457.6 3.9 fusion.118
  473.5 17.4 %collective-permute-start.6 = (bf16[4,1,1440,128]{3,2,1,0:T(8,128)(2,1)}, bf16[4,1,1440,128]{3,2,1,0:T(8,128)(2,1)}, u32[]{:S(2)}, u32[]{:S(2)}) collective-permute-start(bf16[4,1,1440,128]{3,2,1,0:T(8,128)(2,1)} %get-tuple-element.63), channel_id=1, source_target_pairs={{0,1},{1,2},{2,3},{3,4},{4,5},{5,6},{6,7},{8,9},{9,10},{10,11},{11... | collective-permute-start | bytes 4423688 | tf_op jit(solution)/shard_map/ppermute | solution.py:15
  493.8 5.2 fusion.175
  499.1 122.8 %all-reduce.3.cloned.1.call-done = (f32[3,3,128,128]{3,2,1,0:T(8,128)}, f32[3,3,128,69]{2,3,1,0:T(8,128)}) async-done(((f32[3,3,128,128]{3,2,1,0:T(8,128)}, f32[3,3,128,69]{2,3,1,0:T(8,128)}), (f32[3,3,128,128]{3,2,1,0:T(8,128)}, f32[3,3,128,69]{2,3,1,0:T(8,128)})) %all-reduce.3.cloned.1.call-update) | async-done | bytes 907792 | tf_op jit(solution)/shard_map/psum | solution.py:178
  625.5 7.7 %fusion.4 = (bf16[4,4,1441,128]{3,2,1,0:T(8,128)(2,1)S(1)}, bf16[4,4,1441,128]{3,2,1,0:T(8,128)(2,1)S(1)}) fusion(bf16[4,1,1440,128]{3,2,1,0:T(8,128)(2,1)S(1)} %collective-permute-done.7, bf16[4,2,1440,128]{3,2,1,0:T(8,128)(2,1)} %fusion.19, bf16[4,1,1440,128]{3,2,1,0:T(8,128)(2,1)} %collective-permute-done.6), kind=kLoop, calls=%fused_computation.17 | loop fusion | flops 70828032 | bytes 17702912 | tf_op jit(solution)/shard_map/concatenate | solution.py:26
  633.2 3.9 fusion.45
  637.5 3.5 fusion.49
  641.0 3.6 fusion.43
  644.6 3.5 fusion.47
  648.0 3.5 fusion.51
  651.5 4.8 fusion.24
  656.3 3.5 fusion.20
  659.8 19.4 %add_convert_fusion = bf16[4,2,1440,128]{3,2,1,0:T(8,128)(2,1)} fusion(f32[4,2,1440,128]{3,2,1,0:T(8,128)} %fusion.24, f32[4,2,1440,128]{3,2,1,0:T(8,128)} %fusion.43, f32[4,2,1440,128]{3,2,1,0:T(8,128)} %fusion.45, f32[4,2,1440,128]{3,2,1,0:T(8,128)} %fusion.175, f32[4,2,1440,128]{3,2,1,0:T(8,128)} %fusion.47, f32[4,2,1440,128]{3,2,1,0:T(8,128)} %fusion.49, ...), kind=kOutput, calls=%fused_computation.40 | convolution fusion | flops 390758400 | bytes 53116928 | tf_op jit(solution)/shard_map/mrlo,co->mrlc/dot_general | solution.py:92
  (253 shorter events, 136.5 us)
Async XLA Ops:
  7.2 147.7 %copy-start = (f32[69,2,1440]{2,1,0:T(2,128)S(1)}, f32[69,2,1440]{2,1,0:T(2,128)}, u32[]{:S(2)}) copy-start(f32[69,2,1440]{2,1,0:T(2,128)} %param.11) | copy-start | bytes 2384644
  7.2 6.0 copy-start.9
  7.2 6.0 copy-start.21
  9.4 7.3 %collective-permute-start = (bf16[4,1,1440,128]{3,2,1,0:T(8,128)(2,1)S(1)}, bf16[4,1,1440,128]{3,2,1,0:T(8,128)(2,1)S(1)}, u32[]{:S(2)}, u32[]{:S(2)}) collective-permute-start(bf16[4,1,1440,128]{3,2,1,0:T(8,128)(2,1)S(1)} %get-tuple-element.69), channel_id=1, source_target_pairs={{0,1},{1,2},{2,3},{3,4},{4,5},{5,6},{6,7},{8,9},{9,10},{10,11},{11... | collective-permute-start | bytes 4423688 | tf_op jit(solution)/shard_map/ppermute | solution.py:15
  11.9 7.2 %collective-permute-start.1 = (bf16[4,1,1440,128]{3,2,1,0:T(8,128)(2,1)S(1)}, bf16[4,1,1440,128]{3,2,1,0:T(8,128)(2,1)S(1)}, u32[]{:S(2)}, u32[]{:S(2)}) collective-permute-start(bf16[4,1,1440,128]{3,2,1,0:T(8,128)(2,1)S(1)} %get-tuple-element.70), channel_id=1, source_target_pairs={{1,0},{2,1},{3,2},{4,3},{5,4},{6,5},{7,6},{9,8},{10,9},{11,10},{12... | collective-permute-start | bytes 4423688 | tf_op jit(solution)/shard_map/ppermute | solution.py:17
  19.0 22.4 %copy-start.15 = (bf16[4,3,1440,128]{3,2,1,0:T(8,128)(2,1)}, bf16[4,3,1440,128]{3,2,1,0:T(8,128)(2,1)S(1)}, u32[]{:S(2)}) copy-start(bf16[4,3,1440,128]{3,2,1,0:T(8,128)(2,1)S(1)} %get-tuple-element.66) | copy-start | bytes 13271044
  19.6 14.9 %copy-start.2 = (bf16[4,4,1440,128]{3,2,1,0:T(8,128)(2,1)}, bf16[4,4,1440,128]{3,2,1,0:T(8,128)(2,1)S(1)}, u32[]{:S(2)}) copy-start(bf16[4,4,1440,128]{3,2,1,0:T(8,128)(2,1)S(1)} %get-tuple-element.75) | copy-start | bytes 17694724
  19.6 18.3 %copy-start.13 = (bf16[4,3,1440,128]{3,2,1,0:T(8,128)(2,1)}, bf16[4,3,1440,128]{3,2,1,0:T(8,128)(2,1)S(1)}, u32[]{:S(2)}) copy-start(bf16[4,3,1440,128]{3,2,1,0:T(8,128)(2,1)S(1)} %get-tuple-element.76) | copy-start | bytes 13271044
  66.0 34.1 %copy-start.5 = (bf16[4,2,1440,128]{3,2,1,0:T(8,128)(2,1)S(1)}, bf16[4,2,1440,128]{3,2,1,0:T(8,128)(2,1)}, u32[]{:S(2)}) copy-start(bf16[4,2,1440,128]{3,2,1,0:T(8,128)(2,1)} %get-tuple-element.81) | copy-start | bytes 8847364
  66.0 34.1 %copy-start.22 = (bf16[3,3,128,69]{2,3,1,0:T(8,128)(2,1)S(1)}, bf16[3,3,128,69]{2,3,1,0:T(8,128)(2,1)}, u32[]{:S(2)}) copy-start(bf16[3,3,128,69]{2,3,1,0:T(8,128)(2,1)} %param.10) | copy-start | bytes 476932
  68.1 33.7 %collective-permute-start.2 = (bf16[4,1,1440,128]{3,2,1,0:T(8,128)(2,1)S(1)}, bf16[4,1,1440,128]{3,2,1,0:T(8,128)(2,1)S(1)}, u32[]{:S(2)}, u32[]{:S(2)}) collective-permute-start(bf16[4,1,1440,128]{3,2,1,0:T(8,128)(2,1)S(1)} %get-tuple-element.64), channel_id=1, source_target_pairs={{0,1},{1,2},{2,3},{3,4},{4,5},{5,6},{6,7},{8,9},{9,10},{10,11},{11... | collective-permute-start | bytes 4423688 | tf_op jit(solution)/shard_map/ppermute | solution.py:15
  98.5 5.2 collective-permute-start.3
  101.9 29.5 %copy-start.19 = (bf16[4,1,1440,128]{3,2,1,0:T(8,128)(2,1)}, bf16[4,1,1440,128]{3,2,1,0:T(8,128)(2,1)S(1)}, u32[]{:S(2)}) copy-start(bf16[4,1,1440,128]{3,2,1,0:T(8,128)(2,1)S(1)} %collective-permute-done.2) | copy-start | bytes 4423684
  103.7 25.8 %copy-start.17 = (bf16[4,1,1440,128]{3,2,1,0:T(8,128)(2,1)}, bf16[4,1,1440,128]{3,2,1,0:T(8,128)(2,1)S(1)}, u32[]{:S(2)}) copy-start(bf16[4,1,1440,128]{3,2,1,0:T(8,128)(2,1)S(1)} %collective-permute-done.3) | copy-start | bytes 4423684
  111.0 7.7 %copy-start.12 = (bf16[4,4,1441,128]{3,2,1,0:T(8,128)(2,1)}, bf16[4,4,1441,128]{3,2,1,0:T(8,128)(2,1)S(1)}, u32[]{:S(2)}) copy-start(bf16[4,4,1441,128]{3,2,1,0:T(8,128)(2,1)S(1)} %get-tuple-element.56) | copy-start | bytes 17707012
  111.0 22.2 %copy-start.11 = (bf16[4,4,1441,128]{3,2,1,0:T(8,128)(2,1)}, bf16[4,4,1441,128]{3,2,1,0:T(8,128)(2,1)S(1)}, u32[]{:S(2)}) copy-start(bf16[4,4,1441,128]{3,2,1,0:T(8,128)(2,1)S(1)} %get-tuple-element.57) | copy-start | bytes 17707012
  141.4 13.4 %copy-start.26 = (f32[69]{0:T(128)S(1)}, f32[69]{0:T(128)}, u32[]{:S(2)}) copy-start(f32[69]{0:T(128)} %param.13) | copy-start | bytes 832
  141.4 13.4 %copy-start.27 = (f32[69]{0:T(128)S(1)}, f32[69]{0:T(128)}, u32[]{:S(2)}) copy-start(f32[69]{0:T(128)} %param.12) | copy-start | bytes 832
  149.8 51.3 %all-to-all-start = ((bf16[4,69,2,1440]{1,2,0,3:T(2,128)(2,1)}), bf16[4,69,2,1440]{1,2,0,3:T(2,128)(2,1)}, u32[]{:S(2)}, u32[]{:S(2)}) async-start(bf16[4,69,2,1440]{1,2,0,3:T(2,128)(2,1)} %copy.54), calls=%async_computation | async-start | bytes 5898240 | tf_op jit(solution)/shard_map/all_to_all | solution.py:150
  154.7 467.1 %all-reduce.3.cloned.1.call-start = ((), (), s32[]{:S(2)}) async-start(), calls=%async_computation.2 | async-start | bytes 1843200 | tf_op jit(solution)/shard_map/psum | solution.py:178
  212.7 5.6 copy-start.14
  283.4 3.0 copy-start.16
  323.0 2.9 copy-start.6
  323.0 3.1 copy-start.20
  325.7 2.3 slice-start.2
  326.1 2.3 slice-start.3
  326.1 3.7 slice-start.4
  328.4 1.9 slice-start.5
  333.1 25.3 %copy-start.18 = (bf16[4,1,1440,128]{3,2,1,0:T(8,128)(2,1)S(1)}, bf16[4,1,1440,128]{3,2,1,0:T(8,128)(2,1)}, u32[]{:S(2)}) copy-start(bf16[4,1,1440,128]{3,2,1,0:T(8,128)(2,1)} %copy-done.17) | copy-start | bytes 4423684
  334.7 29.3 %collective-permute-start.4 = (bf16[4,69,1,1440]{3,0,2,1:T(4,128)(2,1)S(1)}, bf16[4,69,1,1440]{3,0,2,1:T(4,128)(2,1)S(1)}, u32[]{:S(2)}, u32[]{:S(2)}) collective-permute-start(bf16[4,69,1,1440]{3,0,2,1:T(4,128)(2,1)S(1)} %copy.65), channel_id=1, source_target_pairs={{0,1},{1,2},{2,3},{3,4},{4,5},{5,6},{6,7},{8,9},{9,10},{10,11},{11... | collective-permute-start | bytes 2384648 | tf_op jit(solution)/shard_map/ppermute | solution.py:15
  356.9 50.5 %collective-permute-start.5 = (bf16[4,69,1,1440]{3,0,2,1:T(4,128)(2,1)S(1)}, bf16[4,69,1,1440]{3,0,2,1:T(4,128)(2,1)S(1)}, u32[]{:S(2)}, u32[]{:S(2)}) collective-permute-start(bf16[4,69,1,1440]{3,0,2,1:T(4,128)(2,1)S(1)} %copy.66), channel_id=1, source_target_pairs={{1,0},{2,1},{3,2},{4,3},{5,4},{6,5},{7,6},{9,8},{10,9},{11,10},{12... | collective-permute-start | bytes 2384648 | tf_op jit(solution)/shard_map/ppermute | solution.py:17
  359.1 1.4 copy-start.23
  360.5 3.7 copy-start.25
  407.6 16.8 %copy-start.7 = (bf16[4,69,4,1440]{3,1,2,0:T(8,128)(2,1)}, bf16[4,69,4,1440]{3,1,2,0:T(8,128)(2,1)S(1)}, u32[]{:S(2)}) copy-start(bf16[4,69,4,1440]{3,1,2,0:T(8,128)(2,1)S(1)} %get-tuple-element.78) | copy-start | bytes 9538564
  457.6 4.0 copy-start.3
  457.6 8.6 %slice-start = ((s8[5898240]{0:T(1024)(128)(4,1)}), s8[4194304]{0:T(1024)(128)(4,1)S(1)}, s32[]{:S(2)}) async-start(s8[5898240]{0:T(1024)(128)(4,1)} %bitcast.371), calls=%async_computation.3 | async-start | bytes 8388608
  461.6 4.6 slice-start.1
  467.2 1.8 copy-start.10
  469.1 21.9 %slice-start.6 = ((s8[4423680]{0:T(1024)(128)(4,1)}), s8[4194304]{0:T(1024)(128)(4,1)S(1)}, s32[]{:S(2)}) async-start(s8[4423680]{0:T(1024)(128)(4,1)} %bitcast.377), calls=%async_computation.9 | async-start | bytes 8388608
  470.1 20.8 %slice-start.7 = ((s8[4423680]{0:T(1024)(128)(4,1)}), s8[229376]{0:T(1024)(128)(4,1)S(1)}, s32[]{:S(2)}) async-start(s8[4423680]{0:T(1024)(128)(4,1)} %bitcast.377), calls=%async_computation.10 | async-start | bytes 458752
  472.2 153.3 %collective-permute-start.7 = (bf16[4,1,1440,128]{3,2,1,0:T(8,128)(2,1)}, bf16[4,1,1440,128]{3,2,1,0:T(8,128)(2,1)S(1)}, u32[]{:S(2)}, u32[]{:S(2)}) collective-permute-start(bf16[4,1,1440,128]{3,2,1,0:T(8,128)(2,1)} %get-tuple-element.62), channel_id=1, source_target_pairs={{1,0},{2,1},{3,2},{4,3},{5,4},{6,5},{7,6},{9,8},{10,9},{11,10},{12... | collective-permute-start | bytes 4423688 | tf_op jit(solution)/shard_map/ppermute | solution.py:17
  473.5 152.0 %collective-permute-start.6 = (bf16[4,1,1440,128]{3,2,1,0:T(8,128)(2,1)}, bf16[4,1,1440,128]{3,2,1,0:T(8,128)(2,1)}, u32[]{:S(2)}, u32[]{:S(2)}) collective-permute-start(bf16[4,1,1440,128]{3,2,1,0:T(8,128)(2,1)} %get-tuple-element.63), channel_id=1, source_target_pairs={{0,1},{1,2},{2,3},{3,4},{4,5},{5,6},{6,7},{8,9},{9,10},{10,11},{11... | collective-permute-start | bytes 4423688 | tf_op jit(solution)/shard_map/ppermute | solution.py:15
  493.0 0.8 copy-start.24
  633.2 4.3 copy-start.8
  648.0 3.5 copy-start.4
  659.8 19.4 %copy-start.1 = (f32[69,2,1440]{2,1,0:T(2,128)S(1)}, f32[69,2,1440]{2,1,0:T(2,128)}, u32[]{:S(2)}) copy-start(f32[69,2,1440]{2,1,0:T(2,128)} %param.11) | copy-start | bytes 2384644
Sparse Core Ops, SparseCore 0:
  494.0 127.8 all-reduce.2
where the time goes:
time: 697 us; the launch traced here: 686 us
  waiting for transfers between devices  214 us (31%)
  matrix products  210 us (30%)
  local copies, waits for them, and re-layouts  90.5 us (13%)
  starting transfers between devices  82.9 us (12%)
  other arithmetic  47.9 us (7%)
  blocking collectives  25.7 us (4%)
  between operations  14.9 us (2%)
    psum x1, waiting for transfers between devices, shards(): inner_sum, head_sum = lax.psum((inner_grad, head_grad), ('mem', 'lat'))  123 us
    ppermute x4, starting transfers between devices, padded_2(): lax.ppermute(tail, axis, [(i, (i + 1) % count) for i in range(ends)])  72.5 us
    dot_general x9, matrix products, field_back(): jnp.einsum('mvrl,cv->mrlc', padded_grad[:, :, 2 - row_off:2 - row_off + b...  53.3 us
    dot_general x9, matrix products, hidden_back(): jnp.einsum('mrlo,co->mrlc', padded_grad[:, 2 - row_off:2 - row_off + band...  50.8 us
    dot_general x9, matrix products, hidden_conv(): jnp.einsum('mrlc,co->mrlo', padded[:, row_off:row_off + band_rows, col_of...  49.8 us
    all_to_all x1, waiting for transfers between devices, shards(): lax.all_to_all(field, 'mem', split_axis=3, concat_axis=0, tiled=True)  46 us
    ppermute x4, waiting for transfers between devices, padded_2(): lax.ppermute(head, axis, [((i + 1) % count, i) for i in range(ends)])  44.9 us
    dot_general x9, matrix products, field_conv(): jnp.einsum('mrlc,cv->mvrl', padded[:, row_off:row_off + band_rows, col_of...  32.1 us
  transfers between devices with their start and end apart: 10, of which 4 were waited for; matrix products, arithmetic and copies ran while one was open for 4% of the time, Pallas kernels for 0%

commit v1 on v0

--- a/solution.py
+++ b/solution.py
@@ -2,6 +2,36 @@
 import jax.numpy as jnp
 from jax import lax
 from jax.sharding import PartitionSpec as P
+from jax.lax import axis_index, axis_size, ppermute
+
+
+def _report_regions(original, d_out, s0):
+    b_now = original.shape
+    x_now = jnp.moveaxis(
+        original.reshape(*b_now[:d_out], s0, b_now[d_out] // s0, *b_now[d_out + 1 :]), d_out, 0
+    )
+    return x_now
+
+
+def _number_corner(frame_in, which_dim):
+    oldest = list(frame_in.shape[1:])
+    oldest[which_dim] *= frame_in.shape[0]
+    response = jnp.moveaxis(frame_in, 0, which_dim).reshape(oldest)
+    return response
+
+
+def bench_obtain(unit, axis_name, piece_in, base_x):
+    ready, plain = (axis_size(axis_name), axis_index(axis_name))
+    parts_out = _report_regions(unit, piece_in, ready)
+    kept_rows = [parts_out[plain]]
+    for k in range(1, ready):
+        reached = parts_out[plain ^ k]
+        kept_rows.append(
+            ppermute(reached, axis_name=axis_name, perm=[(dev, dev ^ k) for dev in range(ready)])
+        )
+    parts_out = jnp.stack(kept_rows, axis=0)[plain ^ jnp.arange(ready)]
+    a_next = _number_corner(parts_out, base_x)
+    return a_next
 
 
 def padded_2(cells, sides, width):
@@ -147,7 +177,7 @@
     group = 3
     blocks = variables // group
     inverse_blocks = inverse.reshape(blocks, group)
-    gathered = lax.all_to_all(field, "mem", split_axis=3, concat_axis=0, tiled=True)
+    gathered = bench_obtain(field, "mem", 3, 0)
     values = gathered.astype(jnp.float32)
     members = values.shape[0]
     piece_cells = values.shape[3]

time: 697 us -> 665 us (0.954)
  waiting for transfers between devices: 214 us -> 169 us
  local copies, waits for them, and re-layouts: 90.5 us -> 76.6 us
  matrix products: 210 us -> 218 us
  other arithmetic: 47.9 us -> 55.1 us
  starting transfers between devices: 82.9 us -> 90 us
    all_to_all x1 -> x0, waiting for transfers between devices: 46 us -> none  [shards(): lax.all_to_all(field, 'mem', split_axis=3, concat_axis=0, tiled=True)]
    ppermute x0 -> x3, waiting for transfers between devices: none -> 14.8 us  [bench_obtain(): ppermute(reached, axis_name=axis_name, perm=[(dev, dev ^ k) for dev in ra...]
    ppermute x4, waiting for transfers between devices: 44.9 us -> 31.2 us  [padded_2(): lax.ppermute(head, axis, [((i + 1) % count, i) for i in range(ends)])]
    transpose x3 -> x1, local copies, waits for them, and re-layouts: 13.2 us -> 3.07 us  [split_groups(): return jnp.moveaxis(shaped, 1, 0)]
    convert_element_type x1 -> x0, local copies, waits for them, and re-layouts: 8.43 us -> none  [shards(): field = field_conv(hidden_wrap, conv_head, band_rows).astype(jnp.bfloat16)]
    all_to_all x1 -> x0, local copies, waits for them, and re-layouts: 7.72 us -> none  [shards(): lax.all_to_all(field, 'mem', split_axis=3, concat_axis=0, tiled=True)]
    ppermute x4, starting transfers between devices: 72.5 us -> 80 us  [padded_2(): lax.ppermute(tail, axis, [(i, (i + 1) % count) for i in range(ends)])]
  transfers between devices with their start and end apart: 10 -> 12, of which waited for: 4 -> 6; matrix products, arithmetic and copies ran while one was open for 4% -> 4% of each run, Pallas kernels for 0% -> 0%
where the time goes in v1:
time: 665 us; the launch traced here: 654 us
  matrix products  218 us (33%)
  waiting for transfers between devices  169 us (25%)
  starting transfers between devices  90 us (14%)
  local copies, waits for them, and re-layouts  76.6 us (12%)
  other arithmetic  55.1 us (8%)
  blocking collectives  30.4 us (5%)
  between operations  15.2 us (2%)
    psum x1, waiting for transfers between devices, shards(): inner_sum, head_sum = lax.psum((inner_grad, head_grad), ('mem', 'lat'))  122 us
    ppermute x4, starting transfers between devices, padded_2(): lax.ppermute(tail, axis, [(i, (i + 1) % count) for i in range(ends)])  80 us
    dot_general x9, matrix products, field_back(): jnp.einsum('mvrl,cv->mrlc', padded_grad[:, :, 2 - row_off:2 - row_off + b...  53.1 us
    dot_general x9, matrix products, hidden_back(): jnp.einsum('mrlo,co->mrlc', padded_grad[:, 2 - row_off:2 - row_off + band...  50.8 us
    dot_general x9, matrix products, hidden_conv(): jnp.einsum('mrlc,co->mrlo', padded[:, row_off:row_off + band_rows, col_of...  49.8 us
    dot_general x9, matrix products, field_conv(): jnp.einsum('mrlc,cv->mvrl', padded[:, row_off:row_off + band_rows, col_of...  37.3 us
    ppermute x4, waiting for transfers between devices, padded_2(): lax.ppermute(head, axis, [((i + 1) % count, i) for i in range(ends)])  31.2 us
    all_to_all x1, blocking collectives, shards(): lax.all_to_all(gradient, 'mem', split_axis=0, concat_axis=3, tiled=True)  30.4 us
  transfers between devices with their start and end apart: 12, of which 6 were waited for; matrix products, arithmetic and copies ran while one was open for 4% of the time, Pallas kernels for 0%

profile of v1, /device:TPU:0, one launch (start us, length us, event | category | flops | bytes accessed | tf_op | source)
XLA Modules:
  0.0 654.1 jit_solution(11128416126597448563)
XLA Ops:
  13.2 3.5 fusion.177
  19.7 4.1 fusion.183
  23.8 4.0 fusion.173
  31.2 3.4 fusion.163
  34.6 3.4 fusion.180
  38.0 3.4 fusion.168
  44.8 21.2 %multiply_convert_fusion = (bf16[4,2,1440,128]{3,2,1,0:T(8,128)(2,1)}, f32[4,2,1440,128]{3,2,1,0:T(8,128)}) fusion(bf16[3,3,128,128]{3,2,1,0:T(8,128)(2,1)S(1)} %copy-done.16, bf16[4,4,1,128]{3,2,1,0:T(2,128)(2,1)S(1)} %get-tuple-element.54, bf16[4,4,1440,128]{3,2,1,0:T(8,128)(2,1)} %copy-done.2, f32[4,2,1440,128]{3,2,1,0:T(8,128)} %fusion.168, ...), kind=kOutput, calls=%fused_computation.42 | convolution fusion | flops 408453120 | bytes 61972480 | tf_op jit(solution)/shard_map/mrlc,co->mrlo/dot_general | solution.py:75
  66.1 3.7 fusion.275
  69.8 31.7 %collective-permute-start.2 = (bf16[4,1,1440,128]{3,2,1,0:T(8,128)(2,1)}, bf16[4,1,1440,128]{3,2,1,0:T(8,128)(2,1)}, u32[]{:S(2)}, u32[]{:S(2)}) collective-permute-start(bf16[4,1,1440,128]{3,2,1,0:T(8,128)(2,1)} %get-tuple-element.60), channel_id=1, source_target_pairs={{0,1},{1,2},{2,3},{3,4},{4,5},{5,6},{6,7},{8,9},{9,10},{10,11},{11... | collective-permute-start | bytes 4423688 | tf_op jit(solution)/shard_map/ppermute | solution.py:45
  102.9 3.8 fusion.218
  107.1 9.6 %fusion.7 = (bf16[4,4,1441,128]{3,2,1,0:T(8,128)(2,1)S(1)}, bf16[4,4,1441,128]{3,2,1,0:T(8,128)(2,1)S(1)}) fusion(bf16[4,1,1440,128]{3,2,1,0:T(8,128)(2,1)} %collective-permute-done.3, bf16[4,2,1440,128]{3,2,1,0:T(8,128)(2,1)S(1)} %copy-done.5, bf16[4,1,1440,128]{3,2,1,0:T(8,128)(2,1)} %collective-permute-done.2), kind=kLoop, calls=%fused_computation.27 | loop fusion | flops 70828032 | bytes 17702912 | tf_op jit(solution)/shard_map/concatenate | solution.py:56
  116.7 4.1 fusion.76
  120.7 3.7 fusion.84
  124.4 3.6 fusion.92
  128.0 3.6 fusion.80
  131.7 3.6 fusion.88
  141.6 8.5 %fusion.71 = bf16[4,69,2,1440]{3,1,2,0:T(8,128)(2,1)} fusion(bf16[4,4,1441,128]{3,2,1,0:T(8,128)(2,1)S(1)} %get-tuple-element.53, f32[4,2,1440,69]{2,3,1,0:T(8,128)S(1)} %fusion.53, f32[4,2,1440,69]{2,3,1,0:T(8,128)} %fusion.76, f32[4,2,1440,69]{2,3,1,0:T(8,128)} %fusion.80, f32[4,2,1440,69]{2,3,1,0:T(8,128)S(1)} %fusion.218, ...), kind=kOutput, calls=%fused_computation.110 | convolution fusion | flops 210643200 | bytes 31071744 | tf_op jit(solution)/shard_map/mrlc,cv->mvrl/dot_general | solution.py:89
  150.1 4.2 reshape.58
  154.4 3.6 constant_dynamic-slice_fusion.5
  164.5 7.5 %collective-permute-done.4 = bf16[4,69,2,360]{3,1,2,0:T(8,128)(2,1)S(1)} collective-permute-done((bf16[4,69,2,360]{3,1,2,0:T(8,128)(2,1)}, bf16[4,69,2,360]{3,1,2,0:T(8,128)(2,1)S(1)}, u32[]{:S(2)}, u32[]{:S(2)}) %collective-permute-start.4) | collective-permute-done | bytes 397472 | tf_op jit(solution)/shard_map/ppermute | solution.py:30
  172.0 7.3 %collective-permute-done.5 = bf16[4,69,2,360]{3,1,2,0:T(8,128)(2,1)} collective-permute-done((bf16[4,69,2,360]{3,1,2,0:T(8,128)(2,1)S(1)}, bf16[4,69,2,360]{3,1,2,0:T(8,128)(2,1)}, u32[]{:S(2)}, u32[]{:S(2)}) %collective-permute-start.5) | collective-permute-done | bytes 397472 | tf_op jit(solution)/shard_map/ppermute | solution.py:30
  189.7 61.3 %while.10 = (s32[]{:T(128)}, f32[23,16,3,2,360]{4,1,3,2,0:T(8,128)}, f32[23,16,3,2,360]{4,3,2,0,1:T(2,128)}, f32[23,3]{1,0:T(8,128)S(1)}, s32[]{:T(128)}) while((s32[]{:T(128)}, f32[23,16,3,2,360]{4,1,3,2,0:T(8,128)}, f32[23,16,3,2,360]{4,3,2,0,1:T(2,128)}, f32[23,3]{1,0:T(8,128)S(1)}, s32[]{:T(128)}) %tuple.50), condition=%wide.region_2.3_spmd, body=%wide.region_0.2_spmd.sunk | while | flops 3283202 | bytes 1253493 | solution.py:189
  258.7 30.4 %all_to_all.18 = bf16[16,69,2,360]{3,2,1,0:T(2,128)(2,1)S(1)} all-to-all(bf16[16,69,2,360]{3,2,1,0:T(2,128)(2,1)S(1)} %copy.37), channel_id=1, replica_groups=mesh['mem'=4,'lat'=8] {'mem'}, dimensions={0} | all-to-all | bytes 3179520 | tf_op jit(solution)/shard_map/all_to_all | solution.py:197
  291.9 3.5 all_to_all.16
  307.6 28.2 %collective-permute-start.7 = (bf16[4,69,1,1440]{3,0,2,1:T(4,128)(2,1)S(1)}, bf16[4,69,1,1440]{3,0,2,1:T(4,128)(2,1)S(1)}, u32[]{:S(2)}, u32[]{:S(2)}) collective-permute-start(bf16[4,69,1,1440]{3,0,2,1:T(4,128)(2,1)S(1)} %copy.40), channel_id=1, source_target_pairs={{0,1},{1,2},{2,3},{3,4},{4,5},{5,6},{6,7},{8,9},{9,10},{10,11},{11... | collective-permute-start | bytes 2384648 | tf_op jit(solution)/shard_map/ppermute | solution.py:45
  340.9 3.5 fusion.216
  344.8 30.8 %collective-permute-done.8 = bf16[4,69,1,1440]{3,0,2,1:T(4,128)(2,1)S(1)} collective-permute-done((bf16[4,69,1,1440]{3,0,2,1:T(4,128)(2,1)S(1)}, bf16[4,69,1,1440]{3,0,2,1:T(4,128)(2,1)S(1)}, u32[]{:S(2)}, u32[]{:S(2)}) %collective-permute-start.8) | collective-permute-done | bytes 794912 | tf_op jit(solution)/shard_map/ppermute | solution.py:47
  376.0 4.2 fusion.98
  380.2 4.3 fusion.95
  384.5 4.1 fusion.104
  388.6 4.1 fusion.108
  392.7 4.2 fusion.101
  396.9 3.7 fusion.57
  400.6 3.6 fusion.61
  404.2 21.4 %fusion.19 = bf16[4,2,1440,128]{3,2,1,0:T(8,128)(2,1)} fusion(f32[4,2,1440,128]{3,2,1,0:T(8,128)} %get-tuple-element.82, f32[4,2,1440,128]{3,2,1,0:T(8,128)} %fusion.61, f32[4,2,1440,128]{3,2,1,0:T(8,128)} %fusion.108, f32[4,2,1440,128]{3,2,1,0:T(8,128)} %fusion.95, f32[4,2,1440,128]{3,2,1,0:T(8,128)} %fusion.216, f32[4,2,1440,128]{3,2,1,0:T(8,128)} %fusion.101, ...), kind=kOutput, calls=%fused_computation.40 | convolution fusion | flops 245007360 | bytes 59526144 | tf_op jit(solution)/shard_map/mvrl,cv->mrlc/dot_general | solution.py:103
  425.6 3.9 fusion.118
  441.5 17.5 %collective-permute-start.9 = (bf16[4,1,1440,128]{3,2,1,0:T(8,128)(2,1)}, bf16[4,1,1440,128]{3,2,1,0:T(8,128)(2,1)}, u32[]{:S(2)}, u32[]{:S(2)}) collective-permute-start(bf16[4,1,1440,128]{3,2,1,0:T(8,128)(2,1)} %get-tuple-element.59), channel_id=1, source_target_pairs={{0,1},{1,2},{2,3},{3,4},{4,5},{5,6},{6,7},{8,9},{9,10},{10,11},{11... | collective-permute-start | bytes 4423688 | tf_op jit(solution)/shard_map/ppermute | solution.py:45
  462.0 5.2 fusion.175
  467.2 122.4 %all-reduce.3.cloned.1.call-done = (f32[3,3,128,128]{3,2,1,0:T(8,128)}, f32[3,3,128,69]{2,3,1,0:T(8,128)}) async-done(((f32[3,3,128,128]{3,2,1,0:T(8,128)}, f32[3,3,128,69]{2,3,1,0:T(8,128)}), (f32[3,3,128,128]{3,2,1,0:T(8,128)}, f32[3,3,128,69]{2,3,1,0:T(8,128)})) %all-reduce.3.cloned.1.call-update) | async-done | bytes 907792 | tf_op jit(solution)/shard_map/psum | solution.py:208
  593.3 7.7 %fusion.4 = (bf16[4,4,1441,128]{3,2,1,0:T(8,128)(2,1)S(1)}, bf16[4,4,1441,128]{3,2,1,0:T(8,128)(2,1)S(1)}) fusion(bf16[4,1,1440,128]{3,2,1,0:T(8,128)(2,1)S(1)} %collective-permute-done.10, bf16[4,2,1440,128]{3,2,1,0:T(8,128)(2,1)} %fusion.19, bf16[4,1,1440,128]{3,2,1,0:T(8,128)(2,1)} %collective-permute-done.9), kind=kLoop, calls=%fused_computation.18 | loop fusion | flops 70828032 | bytes 17702912 | tf_op jit(solution)/shard_map/concatenate | solution.py:56
  601.0 3.9 fusion.45
  605.3 3.5 fusion.49
  608.8 3.6 fusion.43
  612.3 3.5 fusion.47
  615.8 3.5 fusion.51
  619.3 4.8 fusion.24
  624.0 3.5 fusion.20
  627.5 19.4 %add_convert_fusion = bf16[4,2,1440,128]{3,2,1,0:T(8,128)(2,1)} fusion(f32[4,2,1440,128]{3,2,1,0:T(8,128)} %fusion.24, f32[4,2,1440,128]{3,2,1,0:T(8,128)} %fusion.43, f32[4,2,1440,128]{3,2,1,0:T(8,128)} %fusion.45, f32[4,2,1440,128]{3,2,1,0:T(8,128)} %fusion.175, f32[4,2,1440,128]{3,2,1,0:T(8,128)} %fusion.47, f32[4,2,1440,128]{3,2,1,0:T(8,128)} %fusion.49, ...), kind=kOutput, calls=%fused_computation.41 | convolution fusion | flops 390758400 | bytes 53116928 | tf_op jit(solution)/shard_map/mrlo,co->mrlc/dot_general | solution.py:122
  (258 shorter events, 148.8 us)
Async XLA Ops:
  7.2 156.3 %copy-start = (f32[69,2,1440]{2,1,0:T(2,128)S(1)}, f32[69,2,1440]{2,1,0:T(2,128)}, u32[]{:S(2)}) copy-start(f32[69,2,1440]{2,1,0:T(2,128)} %param.11) | copy-start | bytes 2384644
  7.2 6.0 copy-start.16
  7.2 582.4 %all-reduce.3.cloned.1.call-start = ((), (), s32[]{:S(2)}) async-start(), calls=%async_computation.1 | async-start | bytes 1843200 | tf_op jit(solution)/shard_map/psum | solution.py:208
  7.2 6.0 copy-start.9
  9.4 7.3 %collective-permute-start = (bf16[4,1,1440,128]{3,2,1,0:T(8,128)(2,1)S(1)}, bf16[4,1,1440,128]{3,2,1,0:T(8,128)(2,1)S(1)}, u32[]{:S(2)}, u32[]{:S(2)}) collective-permute-start(bf16[4,1,1440,128]{3,2,1,0:T(8,128)(2,1)S(1)} %get-tuple-element.65), channel_id=1, source_target_pairs={{0,1},{1,2},{2,3},{3,4},{4,5},{5,6},{6,7},{8,9},{9,10},{10,11},{11... | collective-permute-start | bytes 4423688 | tf_op jit(solution)/shard_map/ppermute | solution.py:45
  11.9 7.2 %collective-permute-start.1 = (bf16[4,1,1440,128]{3,2,1,0:T(8,128)(2,1)S(1)}, bf16[4,1,1440,128]{3,2,1,0:T(8,128)(2,1)S(1)}, u32[]{:S(2)}, u32[]{:S(2)}) collective-permute-start(bf16[4,1,1440,128]{3,2,1,0:T(8,128)(2,1)S(1)} %get-tuple-element.66), channel_id=1, source_target_pairs={{1,0},{2,1},{3,2},{4,3},{5,4},{6,5},{7,6},{9,8},{10,9},{11,10},{12... | collective-permute-start | bytes 4423688 | tf_op jit(solution)/shard_map/ppermute | solution.py:47
  19.0 22.4 %copy-start.14 = (bf16[4,3,1440,128]{3,2,1,0:T(8,128)(2,1)}, bf16[4,3,1440,128]{3,2,1,0:T(8,128)(2,1)S(1)}, u32[]{:S(2)}) copy-start(bf16[4,3,1440,128]{3,2,1,0:T(8,128)(2,1)S(1)} %get-tuple-element.62) | copy-start | bytes 13271044
  19.7 15.0 %copy-start.2 = (bf16[4,4,1440,128]{3,2,1,0:T(8,128)(2,1)}, bf16[4,4,1440,128]{3,2,1,0:T(8,128)(2,1)S(1)}, u32[]{:S(2)}) copy-start(bf16[4,4,1440,128]{3,2,1,0:T(8,128)(2,1)S(1)} %get-tuple-element.75) | copy-start | bytes 17694724
  19.7 18.4 %copy-start.13 = (bf16[4,3,1440,128]{3,2,1,0:T(8,128)(2,1)}, bf16[4,3,1440,128]{3,2,1,0:T(8,128)(2,1)S(1)}, u32[]{:S(2)}) copy-start(bf16[4,3,1440,128]{3,2,1,0:T(8,128)(2,1)S(1)} %get-tuple-element.76) | copy-start | bytes 13271044
  66.1 36.8 %copy-start.19 = (bf16[3,3,128,69]{2,3,1,0:T(8,128)(2,1)S(1)}, bf16[3,3,128,69]{2,3,1,0:T(8,128)(2,1)}, u32[]{:S(2)}) copy-start(bf16[3,3,128,69]{2,3,1,0:T(8,128)(2,1)} %param.10) | copy-start | bytes 476932
  69.8 36.9 %collective-permute-start.2 = (bf16[4,1,1440,128]{3,2,1,0:T(8,128)(2,1)}, bf16[4,1,1440,128]{3,2,1,0:T(8,128)(2,1)}, u32[]{:S(2)}, u32[]{:S(2)}) collective-permute-start(bf16[4,1,1440,128]{3,2,1,0:T(8,128)(2,1)} %get-tuple-element.60), channel_id=1, source_target_pairs={{0,1},{1,2},{2,3},{3,4},{4,5},{5,6},{6,7},{8,9},{9,10},{10,11},{11... | collective-permute-start | bytes 4423688 | tf_op jit(solution)/shard_map/ppermute | solution.py:45
  101.6 5.5 collective-permute-start.3
  102.9 4.2 copy-start.5
  116.6 7.8 %copy-start.12 = (bf16[4,4,1441,128]{3,2,1,0:T(8,128)(2,1)}, bf16[4,4,1441,128]{3,2,1,0:T(8,128)(2,1)S(1)}, u32[]{:S(2)}) copy-start(bf16[4,4,1441,128]{3,2,1,0:T(8,128)(2,1)S(1)} %get-tuple-element.52) | copy-start | bytes 17707012
  116.6 25.0 %copy-start.11 = (bf16[4,4,1441,128]{3,2,1,0:T(8,128)(2,1)}, bf16[4,4,1441,128]{3,2,1,0:T(8,128)(2,1)S(1)}, u32[]{:S(2)}) copy-start(bf16[4,4,1441,128]{3,2,1,0:T(8,128)(2,1)S(1)} %get-tuple-element.53) | copy-start | bytes 17707012
  154.3 9.0 %copy-start.23 = (f32[69]{0:T(128)S(1)}, f32[69]{0:T(128)}, u32[]{:S(2)}) copy-start(f32[69]{0:T(128)} %param.13) | copy-start | bytes 832
  154.4 9.0 %copy-start.24 = (f32[69]{0:T(128)S(1)}, f32[69]{0:T(128)}, u32[]{:S(2)}) copy-start(f32[69]{0:T(128)} %param.12) | copy-start | bytes 832
  158.9 13.1 %collective-permute-start.4 = (bf16[4,69,2,360]{3,1,2,0:T(8,128)(2,1)}, bf16[4,69,2,360]{3,1,2,0:T(8,128)(2,1)S(1)}, u32[]{:S(2)}, u32[]{:S(2)}) collective-permute-start(bf16[4,69,2,360]{3,1,2,0:T(8,128)(2,1)} %bitcast.377), channel_id=1, source_target_pairs={{0,8},{8,0},{16,24},{24,16},{1,9},{9,1},{17,25},{25,17},{2,10},{10... | collective-permute-start | bytes 1192328 | tf_op jit(solution)/shard_map/ppermute | solution.py:30
  160.5 18.8 %collective-permute-start.5 = (bf16[4,69,2,360]{3,1,2,0:T(8,128)(2,1)S(1)}, bf16[4,69,2,360]{3,1,2,0:T(8,128)(2,1)}, u32[]{:S(2)}, u32[]{:S(2)}) collective-permute-start(bf16[4,69,2,360]{3,1,2,0:T(8,128)(2,1)S(1)} %bitcast.401), channel_id=1, source_target_pairs={{0,16},{8,24},{16,0},{24,8},{1,17},{9,25},{17,1},{25,9},{2,18},{10... | collective-permute-start | bytes 1192328 | tf_op jit(solution)/shard_map/ppermute | solution.py:30
  163.1 16.2 %collective-permute-start.6 = (bf16[4,69,2,360]{3,1,2,0:T(8,128)(2,1)S(1)}, bf16[4,69,2,360]{3,1,2,0:T(8,128)(2,1)}, u32[]{:S(2)}, u32[]{:S(2)}) collective-permute-start(bf16[4,69,2,360]{3,1,2,0:T(8,128)(2,1)S(1)} %bitcast.399), channel_id=1, source_target_pairs={{0,24},{8,16},{16,8},{24,0},{1,25},{9,17},{17,9},{25,1},{2,26},{10... | collective-permute-start | bytes 1192328 | tf_op jit(solution)/shard_map/ppermute | solution.py:30
  251.1 3.0 copy-start.15
  251.1 3.0 copy-start.18
  295.4 2.9 copy-start.6
  298.1 2.6 slice-start.2
  298.3 3.0 slice-start.3
  298.3 4.3 slice-start.4
  301.2 1.9 slice-start.5
  307.6 36.9 %collective-permute-start.7 = (bf16[4,69,1,1440]{3,0,2,1:T(4,128)(2,1)S(1)}, bf16[4,69,1,1440]{3,0,2,1:T(4,128)(2,1)S(1)}, u32[]{:S(2)}, u32[]{:S(2)}) collective-permute-start(bf16[4,69,1,1440]{3,0,2,1:T(4,128)(2,1)S(1)} %copy.40), channel_id=1, source_target_pairs={{0,1},{1,2},{2,3},{3,4},{4,5},{5,6},{6,7},{8,9},{9,10},{10,11},{11... | collective-permute-start | bytes 2384648 | tf_op jit(solution)/shard_map/ppermute | solution.py:45
  335.8 39.9 %collective-permute-start.8 = (bf16[4,69,1,1440]{3,0,2,1:T(4,128)(2,1)S(1)}, bf16[4,69,1,1440]{3,0,2,1:T(4,128)(2,1)S(1)}, u32[]{:S(2)}, u32[]{:S(2)}) collective-permute-start(bf16[4,69,1,1440]{3,0,2,1:T(4,128)(2,1)S(1)} %copy.41), channel_id=1, source_target_pairs={{1,0},{2,1},{3,2},{4,3},{5,4},{6,5},{7,6},{9,8},{10,9},{11,10},{12... | collective-permute-start | bytes 2384648 | tf_op jit(solution)/shard_map/ppermute | solution.py:47
  339.5 1.4 copy-start.20
  340.9 3.7 copy-start.22
  375.8 16.8 %copy-start.7 = (bf16[4,69,4,1440]{3,1,2,0:T(8,128)(2,1)}, bf16[4,69,4,1440]{3,1,2,0:T(8,128)(2,1)S(1)}, u32[]{:S(2)}) copy-start(bf16[4,69,4,1440]{3,1,2,0:T(8,128)(2,1)S(1)} %get-tuple-element.78) | copy-start | bytes 9538564
  425.6 3.9 copy-start.3
  425.6 8.5 %slice-start = ((s8[5898240]{0:T(1024)(128)(4,1)}), s8[4194304]{0:T(1024)(128)(4,1)S(1)}, s32[]{:S(2)}) async-start(s8[5898240]{0:T(1024)(128)(4,1)} %bitcast.385), calls=%async_computation.2 | async-start | bytes 8388608
  429.5 4.6 slice-start.1
  435.2 1.8 copy-start.10
  437.0 22.0 %slice-start.6 = ((s8[4423680]{0:T(1024)(128)(4,1)}), s8[4194304]{0:T(1024)(128)(4,1)S(1)}, s32[]{:S(2)}) async-start(s8[4423680]{0:T(1024)(128)(4,1)} %bitcast.391), calls=%async_computation.8 | async-start | bytes 8388608
  438.1 21.0 %slice-start.7 = ((s8[4423680]{0:T(1024)(128)(4,1)}), s8[229376]{0:T(1024)(128)(4,1)S(1)}, s32[]{:S(2)}) async-start(s8[4423680]{0:T(1024)(128)(4,1)} %bitcast.391), calls=%async_computation.9 | async-start | bytes 458752
  440.2 153.1 %collective-permute-start.10 = (bf16[4,1,1440,128]{3,2,1,0:T(8,128)(2,1)}, bf16[4,1,1440,128]{3,2,1,0:T(8,128)(2,1)S(1)}, u32[]{:S(2)}, u32[]{:S(2)}) collective-permute-start(bf16[4,1,1440,128]{3,2,1,0:T(8,128)(2,1)} %get-tuple-element.58), channel_id=1, source_target_pairs={{1,0},{2,1},{3,2},{4,3},{5,4},{6,5},{7,6},{9,8},{10,9},{11,10},{12... | collective-permute-start | bytes 4423688 | tf_op jit(solution)/shard_map/ppermute | solution.py:47
  441.5 151.8 %collective-permute-start.9 = (bf16[4,1,1440,128]{3,2,1,0:T(8,128)(2,1)}, bf16[4,1,1440,128]{3,2,1,0:T(8,128)(2,1)}, u32[]{:S(2)}, u32[]{:S(2)}) collective-permute-start(bf16[4,1,1440,128]{3,2,1,0:T(8,128)(2,1)} %get-tuple-element.59), channel_id=1, source_target_pairs={{0,1},{1,2},{2,3},{3,4},{4,5},{5,6},{6,7},{8,9},{9,10},{10,11},{11... | collective-permute-start | bytes 4423688 | tf_op jit(solution)/shard_map/ppermute | solution.py:45
  460.0 1.9 copy-start.17
  461.1 0.8 copy-start.21
  601.0 4.3 copy-start.8
  615.8 3.5 copy-start.4
  627.5 19.4 %copy-start.1 = (f32[69,2,1440]{2,1,0:T(2,128)S(1)}, f32[69,2,1440]{2,1,0:T(2,128)}, u32[]{:S(2)}) copy-start(f32[69,2,1440]{2,1,0:T(2,128)} %param.11) | copy-start | bytes 2384644
Sparse Core Ops, SparseCore 0:
  462.1 127.5 all-reduce.2
